TPU v7x, 32 devices: a whole 2x2x4 slice. The times are simulated.
32 devices in a mesh: slab: 8 (over z, x), energy: 4 (over y, core).
Axes of the slice: x: 2, y: 2, z: 4, core: 2. Of those that a mesh axis runs over, the one named last changes fastest.
Arguments:
- energy_sq: float32 [4], P('energy'), may hold values from 2.5 to 3.3
- broadening: float32 [4], P('energy'), may hold values from 0.05 to 0.1
- onsite: float32 [8, 192, 192], P('slab'), may hold values from -0.005051815 to 2
- coupling: float32 [8, 192, 192], P('slab'), may hold values from -0.005051815 to 0.005051815
- sigma_in: float32 [4, 8, 192, 384], P('energy', 'slab'), may hold values from -0.02 to 0.005051815
- anharmonic: float32 [8, 192, 192], P('slab'), may hold values from 0.5 to 2
- energy_pairs: int32 [4, 8, 2], P('energy'), may hold values from 0 to 3
Outputs:
- green_diag: float32 [4, 8, 192, 384], P('energy', 'slab')
- sigma_out: float32 [4, 8, 192, 384], P('energy', 'slab')
All inputs are finite; a program needn't handle non-finite values.
Results may differ from a plain program's by a relative error of at most 0.0003.
Values sent between devices are 32-bit elements; how exact they have to be, the bound alone decides.
No kernel may reach another device: no remote copies, remote signals or barrier semaphores. Data moves between devices by JAX's collectives and lax.ppermute only.
A program may use at most 128 MiB of HBM per device.

v0:
```python
import functools

import jax
import jax.numpy as jnp
from jax import lax
from jax.experimental import pallas as pl
from jax.experimental.pallas import tpu as pltpu
from jax.sharding import PartitionSpec as P

HALF = 64
F32 = jnp.float32
BF16 = jnp.bfloat16


def iota(shape, axis):
    return lax.broadcasted_iota(jnp.int32, shape, axis)


def swap(x):
    tiles = [pltpu.roll(x[:, t : t + 128], HALF, 1) for t in range(0, x.shape[1], 128)]
    return tiles[0] if len(tiles) == 1 else jnp.concatenate(tiles, 1)


def times_i(x):
    turned = swap(x)
    return jnp.where((iota(turned.shape, 1) & (2 * HALF - 1)) < HALF, -turned, turned)


def split(x):
    high = x.astype(BF16)
    return high, (x - high.astype(F32)).astype(BF16)


def dot(a, b):
    return jnp.dot(a, b, preferred_element_type=F32)


def dot3(left, right):
    return dot(left[0], right[0]) + (dot(left[0], right[1]) + dot(left[1], right[0]))


def stack_rows(x):
    turned = times_i(x)
    parts = []
    for t in range(0, x.shape[0], HALF):
        parts += [x[t : t + HALF], turned[t : t + HALF]]
    return jnp.concatenate(parts, 0)


def product(left, right):
    return dot3(split(left), split(stack_rows(right)))


def join(parts):
    parts = [p for p in parts if p is not None]
    return jnp.concatenate(parts, 1)


def cut(x, start, stop):
    return x[:, start:stop] if stop > start else None


def row_of(x, s):
    return jnp.broadcast_to(x[s : s + 1, :], (8, 128))


def lane_of(x, k):
    return jnp.take_along_axis(x, jnp.full((8, 128), k, jnp.int32), axis=1)


def cmul(a, b):
    return (a[0] * b[0] - a[1] * b[1], a[0] * b[1] + a[1] * b[0])


def csub(a, b):
    return (a[0] - b[0], a[1] - b[1])


def cadd(a, b):
    return (a[0] + b[0], a[1] + b[1])


def scale_rows(z, u, su):
    return z[0] * u + z[1] * su, z[0] * su - z[1] * u


def invert_small(groups):
    lane = iota((8, 128), 1)
    sub = iota((8, 128), 0)
    sign = jnp.where(lane < HALF, -1.0, 1.0).astype(F32)
    groups = list(groups)
    for g0 in range(8):
        k = 8 * g0
        inside = ((lane & (HALF - 1)) >> 3) == g0
        cols = [(lane_of(groups[g0], k + j), lane_of(groups[g0], HALF + k + j)) for j in range(8)]
        row = groups[g0]
        srow = pltpu.roll(row, HALF, 1) * sign
        row = jnp.where(inside, jnp.where(lane - k == sub, 1.0, 0.0), row)
        srow = jnp.where(inside, jnp.where(lane - HALF - k == sub, 1.0, 0.0), srow)
        others = [
            None
            if g == g0
            else [(lane_of(groups[g], k + j), lane_of(groups[g], HALF + k + j)) for j in range(8)]
            for g in range(8)
        ]
        for i in (0, 2, 4, 6):
            left, right = cols[i], cols[i + 1]
            a = (row_of(left[0], i), row_of(left[1], i))
            c = (row_of(left[0], i + 1), row_of(left[1], i + 1))
            b = (row_of(right[0], i), row_of(right[1], i))
            d = (row_of(right[0], i + 1), row_of(right[1], i + 1))
            det = csub(cmul(a, d), cmul(b, c))
            r = 1.0 / (det[0] * det[0] + det[1] * det[1])
            over = (det[0] * r, -(det[1] * r))
            left = (left[0] - jnp.where(sub == i, 1.0, 0.0), left[1])
            right = (right[0] - jnp.where(sub == i + 1, 1.0, 0.0), right[1])
            for j in range(i + 2, 8):
                x = (row_of(cols[j][0], i), row_of(cols[j][1], i))
                y = (row_of(cols[j][0], i + 1), row_of(cols[j][1], i + 1))
                w1 = cmul(csub(cmul(d, x), cmul(b, y)), over)
                w2 = cmul(csub(cmul(a, y), cmul(c, x)), over)
                cols[j] = csub(cols[j], cadd(cmul(left, w1), cmul(right, w2)))
            x, sx, y, sy = row_of(row, i), row_of(srow, i), row_of(row, i + 1), row_of(srow, i + 1)
            dx, sdx = scale_rows(d, x, sx)
            by, sby = scale_rows(b, y, sy)
            ay, say = scale_rows(a, y, sy)
            cx, scx = scale_rows(c, x, sx)
            w1, sw1 = scale_rows(over, dx - by, sdx - sby)
            w2, sw2 = scale_rows(over, ay - cx, say - scx)
            u1, su1 = scale_rows(left, w1, sw1)
            u2, su2 = scale_rows(right, w2, sw2)
            row = row - (u1 + u2)
            srow = srow - (su1 + su2)
        rows = [(row_of(row, m), row_of(srow, m)) for m in range(8)]
        for g in range(8):
            if g == g0:
                groups[g] = row
                continue
            t = [others[g][m][0] * rows[m][0] + others[g][m][1] * rows[m][1] for m in range(8)]
            total = ((t[0] + t[1]) + (t[2] + t[3])) + ((t[4] + t[5]) + (t[6] + t[7]))
            groups[g] = jnp.where(inside, 0.0, groups[g]) - total
    return groups


def invert_in_place(a_ref):
    width = a_ref.shape[0]
    for k in range(0, width, HALF):
        t = 2 * k
        row = a_ref[k : k + HALF, :]
        turned = times_i(row)
        base = split(jnp.concatenate([jnp.concatenate([row, turned], 1), jnp.concatenate([turned, -row], 1)], 0))
        groups = [a_ref[k + 8 * g : k + 8 * g + 8, t : t + 128] for g in range(8)]
        inverse = jnp.concatenate(invert_small(groups), 0)
        both = dot3(split(inverse), base)
        n = 2 * width
        new_row = join([cut(both, 0, t), inverse, cut(both, t + 128, n)])
        new_turned = join([cut(both, n, n + t), times_i(inverse), cut(both, n + t + 128, 2 * n)])
        right = split(jnp.concatenate([new_row, new_turned], 0))
        for r in range(0, width, HALF):
            if r == k:
                continue
            keep = a_ref[r : r + HALF, :]
            left = split(keep[:, t : t + 128])
            keep = join([cut(keep, 0, t), jnp.zeros((HALF, 128), F32), cut(keep, t + 128, n)])
            a_ref[r : r + HALF, :] = keep - dot3(left, right)
        a_ref[k : k + HALF, :] = new_row


def to_tiles(x):
    low = iota((x.shape[0], 128), 1) < HALF
    t0, t1, t2 = x[:, :128], x[:, 128:256], x[:, 256:]
    middle = pltpu.roll(jnp.where(low, t2, t0), HALF, 1)
    return jnp.concatenate([jnp.where(low, t0, t1), middle, jnp.where(low, t1, t2)], 1)


def from_tiles(x):
    low = iota((x.shape[0], 128), 1) < HALF
    p0, p1, p2 = x[:, :128], x[:, 128:256], x[:, 256:]
    p1 = pltpu.roll(p1, HALF, 1)
    return jnp.concatenate([jnp.where(low, p0, p1), jnp.where(low, p2, p0), jnp.where(low, p1, p2)], 1)


def first_kernel(energy_ref, damping_ref, onsite_ref, sigma_ref, a_ref, x_ref, wide_ref):
    width = onsite_ref.shape[0]
    wide_ref[:, :width] = onsite_ref[...]
    low = iota((width, 128), 1) < HALF
    o0, o1 = wide_ref[:, :128], wide_ref[:, 128:]
    o0, om, o1 = (jnp.where(low, o, 0.0) for o in (o0, pltpu.roll(o0, HALF, 1), o1))
    row = iota((width, 3 * 128), 0)
    lane = iota((width, 3 * 128), 1)
    tile, inner = lane >> 7, lane & 127
    diag = jnp.where(
        row == tile * HALF + inner,
        jnp.where(inner < HALF, energy_ref[0], 0.0),
        jnp.where((row == tile * HALF + inner - HALF) & (inner >= HALF), damping_ref[0], 0.0),
    )
    diag = jnp.where((inner < HALF) | (row == tile * HALF + inner - HALF), diag, 0.0)
    a = diag - jnp.concatenate([o0, om, o1], 1) - to_tiles(sigma_ref[...])
    a_ref[...] = a
    x_ref[...] = a
    invert_in_place(x_ref)


def real_tiles(x, wide_ref):
    width = x.shape[0]
    wide_ref[:, :width] = x
    low = iota((width, 128), 1) < HALF
    o0, o1 = wide_ref[:, :128], wide_ref[:, 128:]
    return jnp.concatenate([jnp.where(low, o, 0.0) for o in (o0, pltpu.roll(o0, HALF, 1), o1)], 1)


def put(out_ref, pair, columns=slice(None)):
    out_ref[0, :, columns] = pair[0]
    out_ref[1, :, columns] = pair[1]


def prepare_kernel(
    energies, slab_ref, pairs_ref, here_ref, swap_a_ref, swap_b_ref, below2_ref,
    left_b_out, left_a_out, right_b_out, right_a_out, weight_out, wide_ref,
):
    width = here_ref.shape[0]
    slab = slab_ref[0]
    odd = (slab & 1) == 1
    eye = jnp.where(iota((width, width), 0) == iota((width, width), 1), 1.0, 0.0)
    a, b = swap_a_ref[...], swap_b_ref[...]
    here = eye + here_ref[...]
    below = eye + jnp.where(odd, a, b)
    above = eye + jnp.where(odd, b, a)
    below2 = jnp.where(slab >= 2, eye + below2_ref[...], 0.0)
    put(left_b_out, split(below.T))
    put(left_a_out, split(here))
    for columns, out, block in (
        (slice(0, 2 * width), right_b_out, below),
        (slice(2 * width, 4 * width), right_b_out, below2.T),
        (slice(0, 2 * width), right_a_out, here.T),
        (slice(2 * width, 4 * width), right_a_out, above),
    ):
        put(out, split(stack_rows(real_tiles(block, wide_ref))), columns)
    count = slab_ref[1]
    for i in range(energies):
        for j in range(i, energies):
            total = jnp.int32(0)
            for p in range(pairs_ref.shape[0]):
                e1, e2 = pairs_ref[p, 0] ^ count, pairs_ref[p, 1] ^ count
                hit = ((e1 == i) & (e2 == j)) | ((e1 == j) & (e2 == i))
                total = total + hit.astype(jnp.int32)
            weight_out[energies * i + j] = jnp.full((8, 128), total.astype(F32))


def pair(ref):
    return ref[0], ref[1]


def second_kernel(
    slab_ref, a_ref, swap_a_ref, swap_b_ref, left_b_ref, left_a_ref, right_b_ref, right_a_ref,
    a_out, l_out, u_out, p_out, x_ref,
):
    n = a_ref.shape[1]
    odd = (slab_ref[0] & 1) == 1
    swap_a, swap_b = swap_a_ref[...], swap_b_ref[...]
    below = dot3(pair(left_b_ref), split(jnp.where(odd, swap_a, swap_b)))
    both = dot3(split(below), pair(right_b_ref))
    above = dot3(pair(left_a_ref), split(jnp.where(odd, swap_b, swap_a)))
    other = dot3(split(above), pair(right_a_ref))
    a = a_ref[...] - both[:, :n] - other[:, :n]
    lower = -both[:, n:]
    upper = -other[:, n:]
    a_out[...] = a
    l_out[...] = lower
    u_out[...] = upper
    x_ref[...] = a
    invert_in_place(x_ref)
    x = split(x_ref[...])
    p_out[0] = dot3(x, split(stack_rows(upper)))
    p_out[1] = dot3(x, split(stack_rows(lower)))


def sides(slab_ref, distance, swap_a_ref, swap_b_ref, i, j):
    low = (slab_ref[0] & distance) == 0
    below = jnp.where(low, swap_b_ref[i], swap_a_ref[i])
    above = jnp.where(low, swap_a_ref[j], swap_b_ref[j])
    return below, above


def middle_kernel(distance, slab_ref, a_ref, l_ref, u_ref, swap_a_ref, swap_b_ref, a_out, l_out, u_out, p_out, x_ref):
    lower, upper = split(l_ref[...]), split(u_ref[...])
    forward, backward = sides(slab_ref, distance, swap_a_ref, swap_b_ref, 0, 1)
    a = a_ref[...] - dot3(lower, split(stack_rows(forward)))
    a = a - dot3(upper, split(stack_rows(backward)))
    backward, forward = sides(slab_ref, distance, swap_a_ref, swap_b_ref, 1, 0)
    new_lower = -dot3(lower, split(stack_rows(backward)))
    new_upper = -dot3(upper, split(stack_rows(forward)))
    a_out[...] = a
    l_out[...] = new_lower
    u_out[...] = new_upper
    x_ref[...] = a
    invert_in_place(x_ref)
    x = split(x_ref[...])
    p_out[0] = dot3(x, split(stack_rows(new_upper)))
    p_out[1] = dot3(x, split(stack_rows(new_lower)))


def pair_kernel(distance, half, slab_ref, a_ref, l_ref, u_ref, swap_a_ref, swap_b_ref, a_out, c_out, w_out, x_ref):
    first = slab_ref[0] < half
    forward, backward = sides(slab_ref, distance, swap_a_ref, swap_b_ref, 0, 1)
    a = a_ref[...] - product(l_ref[...], forward) - product(u_ref[...], backward)
    backward, forward = sides(slab_ref, distance, swap_a_ref, swap_b_ref, 1, 0)
    left = jnp.where(first, u_ref[...], l_ref[...])
    link = -product(left, jnp.where(first, forward, backward))
    a_out[...] = a
    c_out[...] = link
    x_ref[...] = a
    invert_in_place(x_ref)
    w_out[...] = product(x_ref[...], link)


def last_kernel(a_ref, c_ref, w_ref, g_out, x_ref):
    x_ref[...] = a_ref[...] - product(c_ref[...], w_ref[...])
    invert_in_place(x_ref)
    g_out[...] = from_tiles(x_ref[...])


def sigma_kernel(pair_count, weight_ref, scale_ref, *refs):
    green, out_ref, wide_ref = refs[:-2], refs[-2], refs[-1]
    count = len(green)
    width = scale_ref.shape[0]
    wide_ref[:, :width] = scale_ref[...] * (1.0 / pair_count)
    rows = HALF
    low = iota((rows, 128), 1) < HALF

    def weight(i, j):
        return jnp.broadcast_to(weight_ref[count * i + j, :1, :], (rows, 128))

    def combine(z):
        total = None
        for i in range(count):
            inner = None
            for j in range(i, count):
                w = weight(i, j)
                term = (w * z[j][0], w * z[j][1])
                inner = term if inner is None else cadd(inner, term)
            term = cmul(z[i], inner)
            total = term if total is None else cadd(total, term)
        return total

    for r in range(0, width, rows):
        here = slice(r, r + rows)
        main, rest = [], []
        for g in green:
            t0, t1, t2 = g[here, :128], g[here, 128:256], g[here, 256:]
            main.append((t0, pltpu.roll(jnp.where(low, t2, t1), HALF, 1)))
            rest.append((t1, pltpu.roll(t2, HALF, 1)))
        s0, s1 = wide_ref[here, :128], wide_ref[here, 128:]
        m = combine(main)
        q = combine(rest)
        mi = pltpu.roll(m[1] * s0, HALF, 1)
        qi = pltpu.roll(q[1] * s1, HALF, 1)
        out_ref[here, :128] = m[0] * s0
        out_ref[here, 128:256] = jnp.where(low, q[0] * s1, mi)
        out_ref[here, 256:] = jnp.where(low, mi, qi)


def call(kernel, ins, outs, scratch=(), scalars=0):
    vmem = pl.BlockSpec(memory_space=pltpu.VMEM)
    smem = pl.BlockSpec(memory_space=pltpu.SMEM)
    outs = tuple(o if isinstance(o, jax.ShapeDtypeStruct) else jax.ShapeDtypeStruct(o, F32) for o in outs)
    return pl.pallas_call(
        kernel,
        out_shape=outs,
        in_specs=[smem] * scalars + [vmem] * (len(ins) - scalars),
        out_specs=tuple(vmem for _ in outs),
        scratch_shapes=[pltpu.VMEM(s, F32) for s in scratch],
        compiler_params=pltpu.CompilerParams(vmem_limit_bytes=56 * 2**20),
    )(*ins)


def swaps(value, distance):
    count = lax.axis_size("slab")
    near = [(s, s ^ distance) for s in range(count)]
    far = [(s, s + distance if s & distance else s - distance) for s in range(count)]
    far = [(s, t) for s, t in far if 0 <= t < count]
    return lax.ppermute(value, "slab", near), lax.ppermute(value, "slab", far)


def shards(energy_sq, broadening, onsite, coupling, sigma_in, anharmonic, energy_pairs):
    width = onsite.shape[-1]
    block = (width, 2 * width)
    count = lax.axis_size("slab")
    energies = lax.axis_size("energy")
    level_count = count.bit_length() - 1
    slab = lax.axis_index("slab").astype(jnp.int32)
    place = jnp.stack([slab, lax.axis_index("energy").astype(jnp.int32)])
    here = coupling[0]
    bond_a, bond_b = swaps(here, 1)
    a, x0 = call(
        first_kernel, (energy_sq, broadening, onsite[0], sigma_in[0, 0]), (block, block),
        scratch=((width, 256),), scalars=2,
    )
    swap_a, swap_b = swaps(x0, 1)
    here, x0 = lax.optimization_barrier((here, x0))
    below2 = lax.ppermute(here, "slab", [(s, s + 2) for s in range(count - 2)])
    wide = jax.ShapeDtypeStruct((2, 2 * width, 4 * width), BF16)
    real = jax.ShapeDtypeStruct((2, width, width), BF16)
    *operands, weight = call(
        functools.partial(prepare_kernel, energies), (place, energy_pairs[0], here, bond_a, bond_b, below2),
        (real, real, wide, wide, (energies**2, 8, 128)), scratch=((width, 256),), scalars=2,
    )
    a, lower, upper, payload = call(
        second_kernel, (place, a, swap_a, swap_b, *operands),
        (block, block, block, (2,) + block), scratch=(block,), scalars=1,
    )
    for level in range(1, level_count - 1):
        distance = 2**level
        swap_a, swap_b = swaps(payload, distance)
        if level < level_count - 2:
            a, lower, upper, payload = call(
                functools.partial(middle_kernel, distance), (place, a, lower, upper, swap_a, swap_b),
                (block, block, block, (2,) + block), scratch=(block,), scalars=1,
            )
    half = count // 2
    a, link, w = call(
        functools.partial(pair_kernel, half // 2, half), (place, a, lower, upper, swap_a, swap_b),
        (block, block, block), scratch=(block,), scalars=1,
    )
    w = lax.ppermute(w, "slab", [(s, s ^ half) for s in range(count)])
    (green,) = call(last_kernel, (a, link, w), (block,), scratch=(block,))

    table = {0: green}
    step = energies // 2
    while step:
        for offset in list(table):
            table[offset ^ step] = lax.ppermute(
                table[offset], "energy", [(e, e ^ step) for e in range(energies)]
            )
        step //= 2
    (sigma,) = call(
        functools.partial(sigma_kernel, energy_pairs.shape[1]),
        (weight, anharmonic[0], *(table[o] for o in range(energies))), (block,), scratch=((width, 256),),
    )
    return green[None, None], sigma[None, None]


def solution(mesh):
    in_specs = (
        P("energy"),
        P("energy"),
        P("slab", None, None),
        P("slab", None, None),
        P("energy", "slab", None, None),
        P("slab", None, None),
        P("energy", None, None),
    )
    out_specs = (P("energy", "slab", None, None), P("energy", "slab", None, None))
    return jax.shard_map(shards, mesh=mesh, in_specs=in_specs, out_specs=out_specs, check_vma=False)
```

profile of v0, /device:TPU:0, one launch (start us, length us, event | category | flops | bytes accessed | tf_op | source)
XLA Modules:
  0.0 129.7 jit_solution(9566501092849949067)
XLA Ops:
  1.9 9.9 %shard_map.86 = (f32[192,384]{1,0:T(8,128)}, f32[192,384]{1,0:T(8,128)}) custom-call(f32[1]{0:T(128)S(6)} %copy.10.energy_ref, f32[1]{0:T(128)S(6)} %copy.11.damping_ref, f32[192,192]{1,0:T(8,128)} %bitcast.12, f32[192,384]{1,0:T(8,128)} %bitcast.10), custom_call_target="tpu_custom_call" | custom-call | tf_op jit(solution)/shard_map/pallas_call | solution.py:367
  11.8 0.7 collective-permute-start.1
  12.5 5.8 %collective-permute-start = (f32[192,384]{1,0:T(8,128)}, f32[192,384]{1,0:T(8,128)S(1)}, u32[]{:S(2)}, u32[]{:S(2)}) collective-permute-start(f32[192,384]{1,0:T(8,128)} %get-tuple-element.18), channel_id=1, source_target_pairs={{0,4},{4,0},{8,12},{12,8},{16,20},{20,16},{24,28},{28,24},{1,5},{5... | collective-permute-start | bytes 884744 | tf_op jit(solution)/shard_map/ppermute | solution.py:382
  18.3 0.7 collective-permute-start.3
  18.9 4.3 %collective-permute-start.2 = (f32[192,192]{1,0:T(8,128)}, f32[192,192]{1,0:T(8,128)S(1)}, u32[]{:S(2)}, u32[]{:S(2)}) collective-permute-start(f32[192,192]{1,0:T(8,128)} %bitcast.14), channel_id=1, source_target_pairs={{0,4},{4,0},{8,12},{12,8},{16,20},{20,16},{24,28},{28,24},{1,5},{5... | collective-permute-start | bytes 442376 | tf_op jit(solution)/shard_map/ppermute | solution.py:382
  23.3 3.7 %collective-permute-start.4 = (f32[192,192]{1,0:T(8,128)}, f32[192,192]{1,0:T(8,128)S(1)}, u32[]{:S(2)}, u32[]{:S(2)}) collective-permute-start(f32[192,192]{1,0:T(8,128)} %bitcast.15), channel_id=1, source_target_pairs={{0,8},{4,12},{8,16},{12,20},{16,24},{20,28},{1,9},{5,13},{9,17},{1... | collective-permute-start | bytes 442376 | tf_op jit(solution)/shard_map/ppermute | solution.py:401
  27.0 1.3 %copy.9.pairs_ref = s32[8,2]{1,0:T(8,128)} copy(s32[8,2]{0,1:T(2,128)} %bitcast.18) | data formatting | bytes 128 | tf_op jit(solution)/shard_map/squeeze | solution.py:405
  28.3 0.6 pad_add_fusion.slab_ref
  28.9 0.0 collective-permute-done.3.swap_b_ref
  28.9 0.0 copy-start.8
  28.9 10.0 %collective-permute-done.2.swap_a_ref = f32[192,192]{1,0:T(8,128)S(1)} collective-permute-done((f32[192,192]{1,0:T(8,128)}, f32[192,192]{1,0:T(8,128)S(1)}, u32[]{:S(2)}, u32[]{:S(2)}) %collective-permute-start.2) | collective-permute-done | bytes 147488 | tf_op jit(solution)/shard_map/ppermute | solution.py:382
  38.9 0.0 copy-start.9
  38.9 0.0 collective-permute-done.4.below2_ref
  38.9 0.0 copy-done.8
  38.9 0.7 copy-done.9
  39.5 0.0 copy-start.10
  39.5 0.7 copy-done.10
  40.2 3.5 %shard_map.87 = (bf16[2,192,192]{2,1,0:T(8,128)(2,1)}, bf16[2,192,192]{2,1,0:T(8,128)(2,1)}, bf16[2,384,768]{2,1,0:T(8,128)(2,1)}, bf16[2,384,768]{2,1,0:T(8,128)(2,1)}, f32[16,8,128]{2,1,0:T(8,128)}) custom-call(s32[2]{0:T(128)} %pad_add_fusion.slab_ref, s32[8,2]{1,0:T(8,128)} %copy.9.pairs_ref, f32[192,192]{1,0:T(8,128)} %bitcast.16, ...), custom_call_target="tpu_custom_call" | custom-call | tf_op jit(solution)/shard_map/pallas_call | solution.py:367
  43.7 0.0 collective-permute-done.1.swap_b_ref
  43.7 0.0 copy-start.2
  43.7 0.0 collective-permute-done.swap_a_ref
  43.7 0.0 copy-start.3
  43.7 0.7 copy-done.2
  44.4 0.1 copy-done.3
  44.5 13.0 %shard_map.88 = (f32[192,384]{1,0:T(8,128)}, f32[192,384]{1,0:T(8,128)}, f32[192,384]{1,0:T(8,128)}, f32[2,192,384]{2,1,0:T(8,128)}) custom-call(s32[2]{0:T(128)} %pad_add_fusion.slab_ref, f32[192,384]{1,0:T(8,128)} %get-tuple-element.17.a_ref, f32[192,384]{1,0:T(8,128)} %copy-done.3, f32[192,384]{1,0:T(8,128)} %copy-done.2, ...), custom_call_target="tpu_custom_call" | custom-call | tf_op jit(solution)/shard_map/pallas_call | solution.py:367
  57.6 0.9 collective-permute-start.6
  58.5 5.3 %collective-permute-start.5 = (f32[2,192,384]{2,1,0:T(8,128)}, f32[2,192,384]{2,1,0:T(8,128)S(1)}, u32[]{:S(2)}, u32[]{:S(2)}) collective-permute-start(f32[2,192,384]{2,1,0:T(8,128)} %get-tuple-element.27), channel_id=1, source_target_pairs={{0,8},{4,12},{8,0},{12,4},{16,24},{20,28},{24,16},{28,20},{1,9},{5... | collective-permute-start | bytes 1769480 | tf_op jit(solution)/shard_map/ppermute | solution.py:382
  63.8 0.0 collective-permute-done.6.swap_b_ref
  63.8 0.0 copy-start
  63.8 13.4 %collective-permute-done.5.swap_a_ref = f32[2,192,384]{2,1,0:T(8,128)S(1)} collective-permute-done((f32[2,192,384]{2,1,0:T(8,128)}, f32[2,192,384]{2,1,0:T(8,128)S(1)}, u32[]{:S(2)}, u32[]{:S(2)}) %collective-permute-start.5) | collective-permute-done | bytes 589856 | tf_op jit(solution)/shard_map/ppermute | solution.py:382
  77.2 0.0 copy-done
  77.2 0.8 copy-done.1
  78.1 11.4 %shard_map.89 = (f32[192,384]{1,0:T(8,128)}, f32[192,384]{1,0:T(8,128)}, f32[192,384]{1,0:T(8,128)}) custom-call(s32[2]{0:T(128)} %pad_add_fusion.slab_ref, f32[192,384]{1,0:T(8,128)} %get-tuple-element.24.a_ref, f32[192,384]{1,0:T(8,128)} %get-tuple-element.25.l_ref, f32[192,384]{1,0:T(8,128)} %get-tuple-element.26.u_ref, f32[2,192,384]{2,1,0:T(8,128)} %copy-done.1, ...), custom_call_target="tpu_custom_call" | custom-call | tf_op jit(solution)/shard_map/pallas_call | solution.py:367
  89.5 1.6 %collective-permute-start.7 = (f32[192,384]{1,0:T(8,128)}, f32[192,384]{1,0:T(8,128)S(1)}, u32[]{:S(2)}, u32[]{:S(2)}) collective-permute-start(f32[192,384]{1,0:T(8,128)} %get-tuple-element.30), channel_id=1, source_target_pairs={{0,16},{4,20},{8,24},{12,28},{16,0},{20,4},{24,8},{28,12},{1,17},{... | collective-permute-start | bytes 884744 | tf_op jit(solution)/shard_map/ppermute | solution.py:425
  91.1 13.9 %collective-permute-done.7.w_ref = f32[192,384]{1,0:T(8,128)S(1)} collective-permute-done((f32[192,384]{1,0:T(8,128)}, f32[192,384]{1,0:T(8,128)S(1)}, u32[]{:S(2)}, u32[]{:S(2)}) %collective-permute-start.7) | collective-permute-done | bytes 294944 | tf_op jit(solution)/shard_map/ppermute | solution.py:425
  105.0 0.7 copy-done.7
  105.7 10.6 %shard_map.90.refs_0_ = f32[192,384]{1,0:T(8,128)} custom-call(f32[192,384]{1,0:T(8,128)} %get-tuple-element.28.a_ref, f32[192,384]{1,0:T(8,128)} %get-tuple-element.29.c_ref, f32[192,384]{1,0:T(8,128)} %copy-done.7), custom_call_target="tpu_custom_call" | custom-call | tf_op jit(solution)/shard_map/pallas_call | solution.py:367
  116.3 1.5 %collective-permute-start.9 = (f32[192,384]{1,0:T(8,128)}, f32[192,384]{1,0:T(8,128)S(1)}, u32[]{:S(2)}, u32[]{:S(2)}) collective-permute-start(f32[192,384]{1,0:T(8,128)} %shard_map.90.refs_0_), channel_id=1, source_target_pairs={{0,2},{1,3},{2,0},{3,1},{4,6},{5,7},{6,4},{7,5},{8,10},{9,11},{10,... | collective-permute-start | bytes 884744 | tf_op jit(solution)/shard_map/ppermute | solution.py:432
  117.9 0.0 collective-permute-start.8
  117.9 6.7 %collective-permute-done.9.refs_2_ = f32[192,384]{1,0:T(8,128)S(1)} collective-permute-done((f32[192,384]{1,0:T(8,128)}, f32[192,384]{1,0:T(8,128)S(1)}, u32[]{:S(2)}, u32[]{:S(2)}) %collective-permute-start.9) | collective-permute-done | bytes 294944 | tf_op jit(solution)/shard_map/ppermute | solution.py:432
  124.6 0.0 collective-permute-start.10
  124.6 0.0 collective-permute-done.8.refs_1_
  124.6 0.0 copy-start.5
  124.6 1.6 %collective-permute-done.10.refs_3_ = f32[192,384]{1,0:T(8,128)S(1)} collective-permute-done((f32[192,384]{1,0:T(8,128)S(1)}, f32[192,384]{1,0:T(8,128)S(1)}, u32[]{:S(2)}, u32[]{:S(2)}) %collective-permute-start.10) | collective-permute-done | bytes 294944 | tf_op jit(solution)/shard_map/ppermute | solution.py:432
  126.2 0.0 copy-done.4
  126.2 0.0 copy-done.5
  126.2 0.7 copy-done.6
  126.9 2.8 %shard_map.91 = f32[192,384]{1,0:T(8,128)} custom-call(f32[16,8,128]{2,1,0:T(8,128)} %get-tuple-element.31.weight_ref, f32[192,192]{1,0:T(8,128)} %bitcast.17, f32[192,384]{1,0:T(8,128)} %shard_map.90.refs_0_, f32[192,384]{1,0:T(8,128)} %copy-done.5, f32[192,384]{1,0:T(8,128)} %copy-done.4, f32[192,384]{1,0:T(8,128)} %copy-done.6), custom_call_target="tpu_custom_call" | custom-call | tf_op jit(solution)/shard_map/pallas_call | solution.py:367
  (4 shorter events, 0.0 us)
Async XLA Ops:
  11.8 31.9 %collective-permute-start.1 = (f32[192,384]{1,0:T(8,128)}, f32[192,384]{1,0:T(8,128)S(1)}, u32[]{:S(2)}, u32[]{:S(2)}) collective-permute-start(f32[192,384]{1,0:T(8,128)} %get-tuple-element.18), channel_id=1, source_target_pairs={{4,8},{8,4},{12,16},{16,12},{20,24},{24,20},{5,9},{9,5},{13,17},{1... | collective-permute-start | bytes 884744 | tf_op jit(solution)/shard_map/ppermute | solution.py:382
  12.5 31.3 %collective-permute-start = (f32[192,384]{1,0:T(8,128)}, f32[192,384]{1,0:T(8,128)S(1)}, u32[]{:S(2)}, u32[]{:S(2)}) collective-permute-start(f32[192,384]{1,0:T(8,128)} %get-tuple-element.18), channel_id=1, source_target_pairs={{0,4},{4,0},{8,12},{12,8},{16,20},{20,16},{24,28},{28,24},{1,5},{5... | collective-permute-start | bytes 884744 | tf_op jit(solution)/shard_map/ppermute | solution.py:382
  18.3 10.6 %collective-permute-start.3 = (f32[192,192]{1,0:T(8,128)}, f32[192,192]{1,0:T(8,128)S(1)}, u32[]{:S(2)}, u32[]{:S(2)}) collective-permute-start(f32[192,192]{1,0:T(8,128)} %bitcast.13), channel_id=1, source_target_pairs={{4,8},{8,4},{12,16},{16,12},{20,24},{24,20},{5,9},{9,5},{13,17},{1... | collective-permute-start | bytes 442376 | tf_op jit(solution)/shard_map/ppermute | solution.py:382
  18.9 19.9 %collective-permute-start.2 = (f32[192,192]{1,0:T(8,128)}, f32[192,192]{1,0:T(8,128)S(1)}, u32[]{:S(2)}, u32[]{:S(2)}) collective-permute-start(f32[192,192]{1,0:T(8,128)} %bitcast.14), channel_id=1, source_target_pairs={{0,4},{4,0},{8,12},{12,8},{16,20},{20,16},{24,28},{28,24},{1,5},{5... | collective-permute-start | bytes 442376 | tf_op jit(solution)/shard_map/ppermute | solution.py:382
  23.3 15.6 %collective-permute-start.4 = (f32[192,192]{1,0:T(8,128)}, f32[192,192]{1,0:T(8,128)S(1)}, u32[]{:S(2)}, u32[]{:S(2)}) collective-permute-start(f32[192,192]{1,0:T(8,128)} %bitcast.15), channel_id=1, source_target_pairs={{0,8},{4,12},{8,16},{12,20},{16,24},{20,28},{1,9},{5,13},{9,17},{1... | collective-permute-start | bytes 442376 | tf_op jit(solution)/shard_map/ppermute | solution.py:401
  28.9 10.0 %copy-start.8 = (f32[192,192]{1,0:T(8,128)}, f32[192,192]{1,0:T(8,128)S(1)}, u32[]{:S(2)}) copy-start(f32[192,192]{1,0:T(8,128)S(1)} %collective-permute-done.3.swap_b_ref) | copy-start | bytes 442372
  38.9 0.7 copy-start.9
  39.5 0.7 copy-start.10
  43.7 0.7 copy-start.2
  43.7 0.8 copy-start.3
  57.6 6.2 %collective-permute-start.6 = (f32[2,192,384]{2,1,0:T(8,128)}, f32[2,192,384]{2,1,0:T(8,128)S(1)}, u32[]{:S(2)}, u32[]{:S(2)}) collective-permute-start(f32[2,192,384]{2,1,0:T(8,128)} %get-tuple-element.27), channel_id=1, source_target_pairs={{8,16},{12,20},{16,8},{20,12},{9,17},{13,21},{17,9},{21,13},{10,18... | collective-permute-start | bytes 1769480 | tf_op jit(solution)/shard_map/ppermute | solution.py:382
  58.5 18.8 %collective-permute-start.5 = (f32[2,192,384]{2,1,0:T(8,128)}, f32[2,192,384]{2,1,0:T(8,128)S(1)}, u32[]{:S(2)}, u32[]{:S(2)}) collective-permute-start(f32[2,192,384]{2,1,0:T(8,128)} %get-tuple-element.27), channel_id=1, source_target_pairs={{0,8},{4,12},{8,0},{12,4},{16,24},{20,28},{24,16},{28,20},{1,9},{5... | collective-permute-start | bytes 1769480 | tf_op jit(solution)/shard_map/ppermute | solution.py:382
  63.8 13.4 %copy-start = (f32[2,192,384]{2,1,0:T(8,128)}, f32[2,192,384]{2,1,0:T(8,128)S(1)}, u32[]{:S(2)}) copy-start(f32[2,192,384]{2,1,0:T(8,128)S(1)} %collective-permute-done.6.swap_b_ref) | copy-start | bytes 1769476
  77.2 0.8 copy-start.1
  89.5 15.5 %collective-permute-start.7 = (f32[192,384]{1,0:T(8,128)}, f32[192,384]{1,0:T(8,128)S(1)}, u32[]{:S(2)}, u32[]{:S(2)}) collective-permute-start(f32[192,384]{1,0:T(8,128)} %get-tuple-element.30), channel_id=1, source_target_pairs={{0,16},{4,20},{8,24},{12,28},{16,0},{20,4},{24,8},{28,12},{1,17},{... | collective-permute-start | bytes 884744 | tf_op jit(solution)/shard_map/ppermute | solution.py:425
  105.0 0.7 copy-start.7
  116.3 8.2 %collective-permute-start.9 = (f32[192,384]{1,0:T(8,128)}, f32[192,384]{1,0:T(8,128)S(1)}, u32[]{:S(2)}, u32[]{:S(2)}) collective-permute-start(f32[192,384]{1,0:T(8,128)} %shard_map.90.refs_0_), channel_id=1, source_target_pairs={{0,2},{1,3},{2,0},{3,1},{4,6},{5,7},{6,4},{7,5},{8,10},{9,11},{10,... | collective-permute-start | bytes 884744 | tf_op jit(solution)/shard_map/ppermute | solution.py:432
  117.9 6.7 %collective-permute-start.8 = (f32[192,384]{1,0:T(8,128)}, f32[192,384]{1,0:T(8,128)S(1)}, u32[]{:S(2)}, u32[]{:S(2)}) collective-permute-start(f32[192,384]{1,0:T(8,128)} %shard_map.90.refs_0_), channel_id=1, source_target_pairs={{0,1},{1,0},{2,3},{3,2},{4,5},{5,4},{6,7},{7,6},{8,9},{9,8},{10,11... | collective-permute-start | bytes 884744 | tf_op jit(solution)/shard_map/ppermute | solution.py:432
  124.6 1.6 %copy-start.4 = (f32[192,384]{1,0:T(8,128)}, f32[192,384]{1,0:T(8,128)S(1)}, u32[]{:S(2)}) copy-start(f32[192,384]{1,0:T(8,128)S(1)} %collective-permute-done.9.refs_2_) | copy-start | bytes 884740
  124.6 1.6 %collective-permute-start.10 = (f32[192,384]{1,0:T(8,128)S(1)}, f32[192,384]{1,0:T(8,128)S(1)}, u32[]{:S(2)}, u32[]{:S(2)}) collective-permute-start(f32[192,384]{1,0:T(8,128)S(1)} %collective-permute-done.9.refs_2_), channel_id=1, source_target_pairs={{0,1},{1,0},{2,3},{3,2},{4,5},{5,4},{6,7},{7,6},{8,9},{9,8},{10,11... | collective-permute-start | bytes 884744 | tf_op jit(solution)/shard_map/ppermute | solution.py:432
  124.6 1.6 %copy-start.5 = (f32[192,384]{1,0:T(8,128)}, f32[192,384]{1,0:T(8,128)S(1)}, u32[]{:S(2)}) copy-start(f32[192,384]{1,0:T(8,128)S(1)} %collective-permute-done.8.refs_1_) | copy-start | bytes 884740
  126.2 0.7 copy-start.6
where the time goes:
time: 130 us
  Pallas kernels  51.2 us (39%)
  waiting for transfers between devices  45.6 us (35%)
  starting transfers between devices  24.5 us (19%)
  local copies, waits for them, and re-layouts  5.75 us (4%)
  between operations  2.01 us (2%)
    pallas_call x6, Pallas kernels, call(): pl.pallas_call(kernel, out_shape=outs, in_specs=[smem] * scalars + [vmem]...  51.2 us
    ppermute x6, waiting for transfers between devices, swaps(): return (lax.ppermute(value, 'slab', near), lax.ppermute(value, 'slab', far))  23.4 us
    ppermute x6, starting transfers between devices, swaps(): return (lax.ppermute(value, 'slab', near), lax.ppermute(value, 'slab', far))  17.7 us
    ppermute x1, waiting for transfers between devices, shards(): w = lax.ppermute(w, 'slab', [(s, s ^ half) for s in range(count)])  13.9 us
    ppermute x3, waiting for transfers between devices, shards(): lax.ppermute(table[offset], 'energy', [(e, e ^ step) for e in range(energ...  8.29 us
    unnamed x22, local copies, waits for them, and re-layouts  4.41 us
    ppermute x1, starting transfers between devices, shards(): below2 = lax.ppermute(here, 'slab', [(s, s + 2) for s in range(count - 2)])  3.66 us
  transfers between devices with their start and end apart: 11, of which 5 were waited for; matrix products, arithmetic and copies ran while one was open for 1% of the time, Pallas kernels for 3%

commit v1 on v0

--- a/solution.py
+++ b/solution.py
@@ -6,6 +6,7 @@
 from jax.experimental import pallas as pl
 from jax.experimental.pallas import tpu as pltpu
 from jax.sharding import PartitionSpec as P
+
 
 HALF = 64
 F32 = jnp.float32
@@ -360,10 +361,11 @@
         out_ref[here, 256:] = jnp.where(low, mi, qi)
 
 
-def call(kernel, ins, outs, scratch=(), scalars=0):
+def call(kernel, ins, outs, scratch=(), scalars=0, held=0):
+    ins = [keep(x) if scalars <= i < scalars + held else x for i, x in enumerate(ins)]
     vmem = pl.BlockSpec(memory_space=pltpu.VMEM)
     smem = pl.BlockSpec(memory_space=pltpu.SMEM)
-    outs = tuple(o if isinstance(o, jax.ShapeDtypeStruct) else jax.ShapeDtypeStruct(o, F32) for o in outs)
+    outs = tuple(pltpu.VMEM(o, F32) if isinstance(o, tuple) else o for o in outs)
     return pl.pallas_call(
         kernel,
         out_shape=outs,
@@ -374,15 +376,21 @@
     )(*ins)
 
 
+def keep(x):
+    return pltpu.with_memory_space_constraint(x, pltpu.VMEM)
+
+
 def swaps(value, distance):
     count = lax.axis_size("slab")
     near = [(s, s ^ distance) for s in range(count)]
     far = [(s, s + distance if s & distance else s - distance) for s in range(count)]
     far = [(s, t) for s, t in far if 0 <= t < count]
-    return lax.ppermute(value, "slab", near), lax.ppermute(value, "slab", far)
-
-
-def shards(energy_sq, broadening, onsite, coupling, sigma_in, anharmonic, energy_pairs):
+    near = lax.ppermute(value, "slab", near)
+    far = lax.ppermute(value, "slab", far)
+    return keep(near), keep(far)
+
+
+def program(energy_sq, broadening, onsite, coupling, sigma_in, anharmonic, energy_pairs):
     width = onsite.shape[-1]
     block = (width, 2 * width)
     count = lax.axis_size("slab")
@@ -397,17 +405,17 @@
         scratch=((width, 256),), scalars=2,
     )
     swap_a, swap_b = swaps(x0, 1)
-    here, x0 = lax.optimization_barrier((here, x0))
-    below2 = lax.ppermute(here, "slab", [(s, s + 2) for s in range(count - 2)])
-    wide = jax.ShapeDtypeStruct((2, 2 * width, 4 * width), BF16)
-    real = jax.ShapeDtypeStruct((2, width, width), BF16)
+    below2 = keep(lax.ppermute(here, "slab", [(s, s + 2) for s in range(count - 2)]))
+    wide = pltpu.VMEM((2, 2 * width, 4 * width), BF16)
+    real = pltpu.VMEM((2, width, width), BF16)
     *operands, weight = call(
-        functools.partial(prepare_kernel, energies), (place, energy_pairs[0], here, bond_a, bond_b, below2),
+        functools.partial(prepare_kernel, energies),
+        (place, energy_pairs[0], here, bond_a, bond_b, below2),
         (real, real, wide, wide, (energies**2, 8, 128)), scratch=((width, 256),), scalars=2,
     )
     a, lower, upper, payload = call(
         second_kernel, (place, a, swap_a, swap_b, *operands),
-        (block, block, block, (2,) + block), scratch=(block,), scalars=1,
+        (block, block, block, (2,) + block), scratch=(block,), scalars=1, held=7,
     )
     for level in range(1, level_count - 1):
         distance = 2**level
@@ -415,27 +423,29 @@
         if level < level_count - 2:
             a, lower, upper, payload = call(
                 functools.partial(middle_kernel, distance), (place, a, lower, upper, swap_a, swap_b),
-                (block, block, block, (2,) + block), scratch=(block,), scalars=1,
+                (block, block, block, (2,) + block), scratch=(block,), scalars=1, held=5,
             )
     half = count // 2
     a, link, w = call(
         functools.partial(pair_kernel, half // 2, half), (place, a, lower, upper, swap_a, swap_b),
-        (block, block, block), scratch=(block,), scalars=1,
-    )
-    w = lax.ppermute(w, "slab", [(s, s ^ half) for s in range(count)])
-    (green,) = call(last_kernel, (a, link, w), (block,), scratch=(block,))
+        (block, block, block), scratch=(block,), scalars=1, held=5,
+    )
+    w = keep(lax.ppermute(w, "slab", [(s, s ^ half) for s in range(count)]))
+    result = jax.ShapeDtypeStruct(block, F32)
+    (green,) = call(last_kernel, (a, link, w), (result,), scratch=(block,), held=3)
 
     table = {0: green}
     step = energies // 2
     while step:
         for offset in list(table):
-            table[offset ^ step] = lax.ppermute(
-                table[offset], "energy", [(e, e ^ step) for e in range(energies)]
+            table[offset ^ step] = keep(
+                lax.ppermute(table[offset], "energy", [(e, e ^ step) for e in range(energies)])
             )
         step //= 2
     (sigma,) = call(
         functools.partial(sigma_kernel, energy_pairs.shape[1]),
-        (weight, anharmonic[0], *(table[o] for o in range(energies))), (block,), scratch=((width, 256),),
+        (weight, anharmonic[0], *(table[o] for o in range(energies))), (result,),
+        scratch=((width, 256),), held=1,
     )
     return green[None, None], sigma[None, None]
 
@@ -451,4 +461,4 @@
         P("energy", None, None),
     )
     out_specs = (P("energy", "slab", None, None), P("energy", "slab", None, None))
-    return jax.shard_map(shards, mesh=mesh, in_specs=in_specs, out_specs=out_specs, check_vma=False)
+    return jax.shard_map(program, mesh=mesh, in_specs=in_specs, out_specs=out_specs, check_vma=False)

time: 130 us -> 117 us (0.900)
  Pallas kernels: 51.2 us -> 43.6 us
  local copies, waits for them, and re-layouts: 5.75 us -> 1.34 us
    pallas_call x6, Pallas kernels: 51.2 us -> 43.6 us  [call(): pl.pallas_call(kernel, out_shape=outs, in_specs=[smem] * scalars + [vmem]...]
    unnamed x22 -> x0, local copies, waits for them, and re-layouts: 4.41 us -> none
  transfers between devices with their start and end apart: 11 -> 11, of which waited for: 5 -> 5; matrix products, arithmetic and copies ran while one was open for 1% -> 2% of each run, Pallas kernels for 3% -> 2%
where the time goes in v1:
time: 117 us
  waiting for transfers between devices  44.9 us (38%)
  Pallas kernels  43.6 us (37%)
  starting transfers between devices  24.6 us (21%)
  between operations  2 us (2%)
  local copies, waits for them, and re-layouts  1.34 us (1%)
    pallas_call x6, Pallas kernels, call(): pl.pallas_call(kernel, out_shape=outs, in_specs=[smem] * scalars + [vmem]...  43.6 us
    ppermute x3, waiting for transfers between devices, swaps(): near = lax.ppermute(value, 'slab', near)  22.9 us
    ppermute x3, starting transfers between devices, swaps(): near = lax.ppermute(value, 'slab', near)  15.5 us
    ppermute x1, waiting for transfers between devices, program(): w = keep(lax.ppermute(w, 'slab', [(s, s ^ half) for s in range(count)]))  13.6 us
    ppermute x3, waiting for transfers between devices, program(): lax.ppermute(table[offset], 'energy', [(e, e ^ step) for e in range(energ...  8.29 us
    ppermute x1, starting transfers between devices, program(): lax.ppermute(here, 'slab', [(s, s + 2) for s in range(count - 2)])  3.48 us
    ppermute x3, starting transfers between devices, swaps(): far = lax.ppermute(value, 'slab', far)  2.45 us
  transfers between devices with their start and end apart: 11, of which 5 were waited for; matrix products, arithmetic and copies ran while one was open for 2% of the time, Pallas kernels for 2%

profile of v1, /device:TPU:0, one launch (start us, length us, event | category | flops | bytes accessed | tf_op | source)
XLA Modules:
  0.0 117.1 jit_solution(5720684507861447721)
XLA Ops:
  1.9 9.2 %shard_map.86 = (f32[192,384]{1,0:T(8,128)S(1)}, f32[192,384]{1,0:T(8,128)S(1)}) custom-call(f32[1]{0:T(128)S(6)} %copy.10.energy_ref, f32[1]{0:T(128)S(6)} %copy.11.damping_ref, f32[192,192]{1,0:T(8,128)} %bitcast.12, f32[192,384]{1,0:T(8,128)} %bitcast.10), custom_call_target="tpu_custom_call" | custom-call | tf_op jit(solution)/shard_map/pallas_call | solution.py:369
  11.1 0.7 collective-permute-start.1
  11.8 5.8 %collective-permute-start = (f32[192,384]{1,0:T(8,128)S(1)}, f32[192,384]{1,0:T(8,128)S(1)}, u32[]{:S(2)}, u32[]{:S(2)}) collective-permute-start(f32[192,384]{1,0:T(8,128)S(1)} %get-tuple-element.17), channel_id=1, source_target_pairs={{0,4},{4,0},{8,12},{12,8},{16,20},{20,16},{24,28},{28,24},{1,5},{5... | collective-permute-start | bytes 884744 | tf_op jit(solution)/shard_map/ppermute | solution.py:388
  17.6 3.5 %collective-permute-start.4 = (f32[192,192]{1,0:T(8,128)}, f32[192,192]{1,0:T(8,128)S(1)}, u32[]{:S(2)}, u32[]{:S(2)}) collective-permute-start(f32[192,192]{1,0:T(8,128)} %bitcast.13), channel_id=1, source_target_pairs={{0,8},{4,12},{8,16},{12,20},{16,24},{20,28},{1,9},{5,13},{9,17},{1... | collective-permute-start | bytes 442376 | tf_op jit(solution)/shard_map/ppermute | solution.py:408
  21.1 0.9 collective-permute-start.3
  21.9 4.3 %collective-permute-start.2 = (f32[192,192]{1,0:T(8,128)}, f32[192,192]{1,0:T(8,128)S(1)}, u32[]{:S(2)}, u32[]{:S(2)}) collective-permute-start(f32[192,192]{1,0:T(8,128)} %bitcast.15), channel_id=1, source_target_pairs={{0,4},{4,0},{8,12},{12,8},{16,20},{20,16},{24,28},{28,24},{1,5},{5... | collective-permute-start | bytes 442376 | tf_op jit(solution)/shard_map/ppermute | solution.py:388
  26.3 1.3 %copy.9.pairs_ref = s32[8,2]{1,0:T(8,128)} copy(s32[8,2]{0,1:T(2,128)} %bitcast.18) | data formatting | bytes 128 | tf_op jit(solution)/shard_map/squeeze | solution.py:413
  27.6 0.6 pad_add_fusion.slab_ref
  28.3 0.0 collective-permute-done.4.below2_ref
  28.3 0.0 collective-permute-done.3.swap_b_ref
  28.3 9.7 %collective-permute-done.2.swap_a_ref = f32[192,192]{1,0:T(8,128)S(1)} collective-permute-done((f32[192,192]{1,0:T(8,128)}, f32[192,192]{1,0:T(8,128)S(1)}, u32[]{:S(2)}, u32[]{:S(2)}) %collective-permute-start.2) | collective-permute-done | bytes 147488 | tf_op jit(solution)/shard_map/ppermute | solution.py:388
  38.0 1.9 %shard_map.87 = (bf16[2,192,192]{2,1,0:T(8,128)(2,1)S(1)}, bf16[2,192,192]{2,1,0:T(8,128)(2,1)S(1)}, bf16[2,384,768]{2,1,0:T(8,128)(2,1)S(1)}, bf16[2,384,768]{2,1,0:T(8,128)(2,1)S(1)}, f32[16,8,128]{2,1,0:T(8,128)S(1)}) custom-call(s32[2]{0:T(128)} %pad_add_fusion.slab_ref, s32[8,2]{1,0:T(8,128)} %copy.9.pairs_ref, f32[192,192]{1,0:T(8,128)} %bitcast.16, ...), custom_call_target="tpu_custom_call" | custom-call | tf_op jit(solution)/shard_map/pallas_call | solution.py:369
  39.8 0.0 collective-permute-done.1.swap_b_ref
  39.9 0.0 collective-permute-done.swap_a_ref
  39.9 10.8 %shard_map.88 = (f32[192,384]{1,0:T(8,128)S(1)}, f32[192,384]{1,0:T(8,128)S(1)}, f32[192,384]{1,0:T(8,128)S(1)}, f32[2,192,384]{2,1,0:T(8,128)S(1)}) custom-call(s32[2]{0:T(128)} %pad_add_fusion.slab_ref, f32[192,384]{1,0:T(8,128)S(1)} %get-tuple-element.16.a_ref, f32[192,384]{1,0:T(8,128)S(1)} %collective-permute-done.swap_a_ref, ...), custom_call_target="tpu_custom_call" | custom-call | tf_op jit(solution)/shard_map/pallas_call | solution.py:369
  50.7 0.9 collective-permute-start.6
  51.6 5.3 %collective-permute-start.5 = (f32[2,192,384]{2,1,0:T(8,128)S(1)}, f32[2,192,384]{2,1,0:T(8,128)S(1)}, u32[]{:S(2)}, u32[]{:S(2)}) collective-permute-start(f32[2,192,384]{2,1,0:T(8,128)S(1)} %get-tuple-element.25), channel_id=1, source_target_pairs={{0,8},{4,12},{8,0},{12,4},{16,24},{20,28},{24,16},{28,20},{1,9},{5... | collective-permute-start | bytes 1769480 | tf_op jit(solution)/shard_map/ppermute | solution.py:388
  56.9 0.0 collective-permute-done.6.swap_b_ref
  56.9 13.2 %collective-permute-done.5.swap_a_ref = f32[2,192,384]{2,1,0:T(8,128)S(1)} collective-permute-done((f32[2,192,384]{2,1,0:T(8,128)S(1)}, f32[2,192,384]{2,1,0:T(8,128)S(1)}, u32[]{:S(2)}, u32[]{:S(2)}) %collective-permute-start.5) | collective-permute-done | bytes 589856 | tf_op jit(solution)/shard_map/ppermute | solution.py:388
  70.1 9.8 %shard_map.89 = (f32[192,384]{1,0:T(8,128)S(1)}, f32[192,384]{1,0:T(8,128)S(1)}, f32[192,384]{1,0:T(8,128)S(1)}) custom-call(s32[2]{0:T(128)} %pad_add_fusion.slab_ref, f32[192,384]{1,0:T(8,128)S(1)} %get-tuple-element.22.a_ref, f32[192,384]{1,0:T(8,128)S(1)} %get-tuple-element.23.l_ref, f32[192,384]{1,0:T(8,128)S(1)} %get-tuple-element.24.u_ref, ...), custom_call_target="tpu_custom_call" | custom-call | tf_op jit(solution)/shard_map/pallas_call | solution.py:369
  80.0 1.7 %collective-permute-start.7 = (f32[192,384]{1,0:T(8,128)S(1)}, f32[192,384]{1,0:T(8,128)S(1)}, u32[]{:S(2)}, u32[]{:S(2)}) collective-permute-start(f32[192,384]{1,0:T(8,128)S(1)} %get-tuple-element.28), channel_id=1, source_target_pairs={{0,16},{4,20},{8,24},{12,28},{16,0},{20,4},{24,8},{28,12},{1,17},{... | collective-permute-start | bytes 884744 | tf_op jit(solution)/shard_map/ppermute | solution.py:433
  81.7 13.6 %collective-permute-done.7.w_ref = f32[192,384]{1,0:T(8,128)S(1)} collective-permute-done((f32[192,384]{1,0:T(8,128)S(1)}, f32[192,384]{1,0:T(8,128)S(1)}, u32[]{:S(2)}, u32[]{:S(2)}) %collective-permute-start.7) | collective-permute-done | bytes 294944 | tf_op jit(solution)/shard_map/ppermute | solution.py:433
  95.3 9.5 %shard_map.90.refs_0_ = f32[192,384]{1,0:T(8,128)} custom-call(f32[192,384]{1,0:T(8,128)S(1)} %get-tuple-element.26.a_ref, f32[192,384]{1,0:T(8,128)S(1)} %get-tuple-element.27.c_ref, f32[192,384]{1,0:T(8,128)S(1)} %collective-permute-done.7.w_ref), custom_call_target="tpu_custom_call" | custom-call | tf_op jit(solution)/shard_map/pallas_call | solution.py:369
  104.8 1.5 %collective-permute-start.9 = (f32[192,384]{1,0:T(8,128)}, f32[192,384]{1,0:T(8,128)S(1)}, u32[]{:S(2)}, u32[]{:S(2)}) collective-permute-start(f32[192,384]{1,0:T(8,128)} %shard_map.90.refs_0_), channel_id=1, source_target_pairs={{0,2},{1,3},{2,0},{3,1},{4,6},{5,7},{6,4},{7,5},{8,10},{9,11},{10,... | collective-permute-start | bytes 884744 | tf_op jit(solution)/shard_map/ppermute | solution.py:442
  106.3 0.0 collective-permute-start.8
  106.3 6.7 %collective-permute-done.9.refs_2_ = f32[192,384]{1,0:T(8,128)S(1)} collective-permute-done((f32[192,384]{1,0:T(8,128)}, f32[192,384]{1,0:T(8,128)S(1)}, u32[]{:S(2)}, u32[]{:S(2)}) %collective-permute-start.9) | collective-permute-done | bytes 294944 | tf_op jit(solution)/shard_map/ppermute | solution.py:442
  113.1 0.0 collective-permute-start.10
  113.1 0.0 collective-permute-done.8.refs_1_
  113.1 1.6 %collective-permute-done.10.refs_3_ = f32[192,384]{1,0:T(8,128)S(1)} collective-permute-done((f32[192,384]{1,0:T(8,128)S(1)}, f32[192,384]{1,0:T(8,128)S(1)}, u32[]{:S(2)}, u32[]{:S(2)}) %collective-permute-start.10) | collective-permute-done | bytes 294944 | tf_op jit(solution)/shard_map/ppermute | solution.py:442
  114.6 2.5 %shard_map.91 = f32[192,384]{1,0:T(8,128)} custom-call(f32[16,8,128]{2,1,0:T(8,128)S(1)} %get-tuple-element.29.weight_ref, f32[192,192]{1,0:T(8,128)} %bitcast.17, f32[192,384]{1,0:T(8,128)} %shard_map.90.refs_0_, f32[192,384]{1,0:T(8,128)S(1)} %collective-permute-done.8.refs_1_, f32[192,384]{1,0:T(8,128)S(1)} %collective-permute-done.9.refs_2_, ...), custom_call_target="tpu_custom_call" | custom-call | tf_op jit(solution)/shard_map/pallas_call | solution.py:369
Async XLA Ops:
  11.1 28.8 %collective-permute-start.1 = (f32[192,384]{1,0:T(8,128)S(1)}, f32[192,384]{1,0:T(8,128)S(1)}, u32[]{:S(2)}, u32[]{:S(2)}) collective-permute-start(f32[192,384]{1,0:T(8,128)S(1)} %get-tuple-element.17), channel_id=1, source_target_pairs={{4,8},{8,4},{12,16},{16,12},{20,24},{24,20},{5,9},{9,5},{13,17},{1... | collective-permute-start | bytes 884744 | tf_op jit(solution)/shard_map/ppermute | solution.py:389
  11.8 28.1 %collective-permute-start = (f32[192,384]{1,0:T(8,128)S(1)}, f32[192,384]{1,0:T(8,128)S(1)}, u32[]{:S(2)}, u32[]{:S(2)}) collective-permute-start(f32[192,384]{1,0:T(8,128)S(1)} %get-tuple-element.17), channel_id=1, source_target_pairs={{0,4},{4,0},{8,12},{12,8},{16,20},{20,16},{24,28},{28,24},{1,5},{5... | collective-permute-start | bytes 884744 | tf_op jit(solution)/shard_map/ppermute | solution.py:388
  17.6 10.7 %collective-permute-start.4 = (f32[192,192]{1,0:T(8,128)}, f32[192,192]{1,0:T(8,128)S(1)}, u32[]{:S(2)}, u32[]{:S(2)}) collective-permute-start(f32[192,192]{1,0:T(8,128)} %bitcast.13), channel_id=1, source_target_pairs={{0,8},{4,12},{8,16},{12,20},{16,24},{20,28},{1,9},{5,13},{9,17},{1... | collective-permute-start | bytes 442376 | tf_op jit(solution)/shard_map/ppermute | solution.py:408
  21.1 7.2 %collective-permute-start.3 = (f32[192,192]{1,0:T(8,128)}, f32[192,192]{1,0:T(8,128)S(1)}, u32[]{:S(2)}, u32[]{:S(2)}) collective-permute-start(f32[192,192]{1,0:T(8,128)} %bitcast.14), channel_id=1, source_target_pairs={{4,8},{8,4},{12,16},{16,12},{20,24},{24,20},{5,9},{9,5},{13,17},{1... | collective-permute-start | bytes 442376 | tf_op jit(solution)/shard_map/ppermute | solution.py:389
  21.9 16.0 %collective-permute-start.2 = (f32[192,192]{1,0:T(8,128)}, f32[192,192]{1,0:T(8,128)S(1)}, u32[]{:S(2)}, u32[]{:S(2)}) collective-permute-start(f32[192,192]{1,0:T(8,128)} %bitcast.15), channel_id=1, source_target_pairs={{0,4},{4,0},{8,12},{12,8},{16,20},{20,16},{24,28},{28,24},{1,5},{5... | collective-permute-start | bytes 442376 | tf_op jit(solution)/shard_map/ppermute | solution.py:388
  50.7 6.2 %collective-permute-start.6 = (f32[2,192,384]{2,1,0:T(8,128)S(1)}, f32[2,192,384]{2,1,0:T(8,128)S(1)}, u32[]{:S(2)}, u32[]{:S(2)}) collective-permute-start(f32[2,192,384]{2,1,0:T(8,128)S(1)} %get-tuple-element.25), channel_id=1, source_target_pairs={{8,16},{12,20},{16,8},{20,12},{9,17},{13,21},{17,9},{21,13},{10,18... | collective-permute-start | bytes 1769480 | tf_op jit(solution)/shard_map/ppermute | solution.py:389
  51.6 18.5 %collective-permute-start.5 = (f32[2,192,384]{2,1,0:T(8,128)S(1)}, f32[2,192,384]{2,1,0:T(8,128)S(1)}, u32[]{:S(2)}, u32[]{:S(2)}) collective-permute-start(f32[2,192,384]{2,1,0:T(8,128)S(1)} %get-tuple-element.25), channel_id=1, source_target_pairs={{0,8},{4,12},{8,0},{12,4},{16,24},{20,28},{24,16},{28,20},{1,9},{5... | collective-permute-start | bytes 1769480 | tf_op jit(solution)/shard_map/ppermute | solution.py:388
  80.0 15.4 %collective-permute-start.7 = (f32[192,384]{1,0:T(8,128)S(1)}, f32[192,384]{1,0:T(8,128)S(1)}, u32[]{:S(2)}, u32[]{:S(2)}) collective-permute-start(f32[192,384]{1,0:T(8,128)S(1)} %get-tuple-element.28), channel_id=1, source_target_pairs={{0,16},{4,20},{8,24},{12,28},{16,0},{20,4},{24,8},{28,12},{1,17},{... | collective-permute-start | bytes 884744 | tf_op jit(solution)/shard_map/ppermute | solution.py:433
  104.8 8.2 %collective-permute-start.9 = (f32[192,384]{1,0:T(8,128)}, f32[192,384]{1,0:T(8,128)S(1)}, u32[]{:S(2)}, u32[]{:S(2)}) collective-permute-start(f32[192,384]{1,0:T(8,128)} %shard_map.90.refs_0_), channel_id=1, source_target_pairs={{0,2},{1,3},{2,0},{3,1},{4,6},{5,7},{6,4},{7,5},{8,10},{9,11},{10,... | collective-permute-start | bytes 884744 | tf_op jit(solution)/shard_map/ppermute | solution.py:442
  106.3 6.7 %collective-permute-start.8 = (f32[192,384]{1,0:T(8,128)}, f32[192,384]{1,0:T(8,128)S(1)}, u32[]{:S(2)}, u32[]{:S(2)}) collective-permute-start(f32[192,384]{1,0:T(8,128)} %shard_map.90.refs_0_), channel_id=1, source_target_pairs={{0,1},{1,0},{2,3},{3,2},{4,5},{5,4},{6,7},{7,6},{8,9},{9,8},{10,11... | collective-permute-start | bytes 884744 | tf_op jit(solution)/shard_map/ppermute | solution.py:442
  113.1 1.6 %collective-permute-start.10 = (f32[192,384]{1,0:T(8,128)S(1)}, f32[192,384]{1,0:T(8,128)S(1)}, u32[]{:S(2)}, u32[]{:S(2)}) collective-permute-start(f32[192,384]{1,0:T(8,128)S(1)} %collective-permute-done.9.refs_2_), channel_id=1, source_target_pairs={{0,1},{1,0},{2,3},{3,2},{4,5},{5,4},{6,7},{7,6},{8,9},{9,8},{10,11... | collective-permute-start | bytes 884744 | tf_op jit(solution)/shard_map/ppermute | solution.py:442
